TPU v7x, 32 devices: a whole 2x2x4 slice. The times are simulated.
32 devices in a mesh: ang: 16 (over z, x, core), strip: 2 (over y).
Axes of the slice: x: 2, y: 2, z: 4, core: 2. Of those that a mesh axis runs over, the one named last changes fastest.
Arguments:
- measured: float32 [16, 16, 128, 128], P('ang', 'strip'), may hold values from 0.05 to 4
- positions: int32 [16, 16], P('ang', 'strip'), may hold values from 0 to 384
- probe_field: float32 [2, 128, 128], replicated, may hold values from -6 to 6
- object_field: float32 [16, 512, 2, 128], P('ang', 'strip'), may hold values from -6 to 6
- dual_field: float32 [16, 512, 2, 128], P('ang', 'strip'), may hold values from -6 to 6
- volume: float32 [8192, 2, 128], P(('ang', 'strip')), may hold values from -6 to 6
- radon_tiles: bfloat16 [32, 16, 2, 32, 256], P(('ang', 'strip')), may hold values from -0.1875 to 0.1875
- tile_range: int32 [16, 16, 2, 1], P('ang', None, 'strip'), may hold values from 0 to 14
Outputs:
- object_next: float32 [16, 512, 2, 128], P('ang', 'strip')
- dual_next: float32 [16, 512, 2, 128], P('ang', 'strip')
- volume_next: float32 [8192, 2, 128], P(('ang', 'strip'))
Inputs may be any that keep to these rules, and one draw needn't show every extreme that they name: `positions`: a frame covers 128 detector columns from its position. A pixel tile meets ray tiles tile_range to tile_range + 1 at that angle.
All inputs are finite; a program needn't handle non-finite values.
Results may differ from a plain program's by a relative error of at most 0.0027.
Values may be sent and summed in bfloat16 or wider, within the bound.
A program may use at most 64 MiB of HBM per device.

v0:
```python
import math

import jax
import jax.numpy as jnp
from jax import lax
from jax.sharding import PartitionSpec as P

PROBE = 128
NZ = 128
NDET = 512
RAYS = 32
TILE = 256
HITS = 2
PT_DEV = 1
NR = 16


penalty = 1.0
object_step = 0.1
volume_step = 1.0
precise = lax.Precision.HIGHEST


def dft_tables(length):
    indices = jnp.arange(length, dtype=jnp.int32)
    phases = indices[:, None] * indices[None, :] % length
    angles = phases.astype(jnp.float32) * (2.0 * math.pi / length)
    scaling = 1.0 / math.sqrt(length)
    return (jnp.cos(angles) * scaling, jnp.sin(angles) * scaling)


def transform(real_part, imag_part, cosine_table, sine_table, handed):
    left_re = jnp.einsum(
        "kc,fcr->fkr", cosine_table, real_part, precision=precise
    ) + handed * jnp.einsum("kc,fcr->fkr", sine_table, imag_part, precision=precise)
    left_im = jnp.einsum(
        "kc,fcr->fkr", cosine_table, imag_part, precision=precise
    ) - handed * jnp.einsum("kc,fcr->fkr", sine_table, real_part, precision=precise)
    out_re = jnp.einsum(
        "fkr,rl->fkl", left_re, cosine_table, precision=precise
    ) + handed * jnp.einsum("fkr,rl->fkl", left_im, sine_table, precision=precise)
    out_im = jnp.einsum(
        "fkr,rl->fkl", left_im, cosine_table, precision=precise
    ) - handed * jnp.einsum("fkr,rl->fkl", left_re, sine_table, precision=precise)
    return (out_re, out_im)


def intersection_gradient(intensity, starts, field, probe_field, cosine_table, sine_table):
    window = probe_field.shape[1]

    def cutout(start):
        return lax.dynamic_slice_in_dim(field, start, window, 0)

    patches = jax.vmap(cutout)(starts)
    object_re = patches[:, :, 0, :]
    object_im = patches[:, :, 1, :]
    probe_re = probe_field[0]
    probe_im = probe_field[1]
    wave_re = probe_re * object_re - probe_im * object_im
    wave_im = probe_re * object_im + probe_im * object_re
    far_re, far_im = transform(wave_re, wave_im, cosine_table, sine_table, 1.0)
    modulus = jnp.sqrt(far_re * far_re + far_im * far_im)
    shrink = 1.0 - jnp.sqrt(intensity) / jnp.maximum(modulus, 1.0)
    back_re, back_im = transform(far_re * shrink, far_im * shrink, cosine_table, sine_table, -1.0)
    grad_re = probe_re * back_re + probe_im * back_im
    grad_im = probe_re * back_im - probe_im * back_re
    frame_grads = jnp.stack([grad_re, grad_im], axis=2)

    def deposit(index, total):
        piece = lax.dynamic_slice_in_dim(total, starts[index], window, 0)
        return lax.dynamic_update_slice_in_dim(total, piece + frame_grads[index], starts[index], 0)

    return lax.fori_loop(0, starts.shape[0], deposit, jnp.zeros(field.shape, jnp.float32))


def body(
    measured, positions, probe_field, object_field, dual_field, volume, radon_tiles, tile_range
):
    angles = lax.axis_size("ang")
    range_ids = jnp.arange(NR, dtype=jnp.int32)
    hit_offsets = jnp.arange(HITS, dtype=jnp.int32)
    targets_flat = (tile_range.reshape(angles * PT_DEV, 1) + hit_offsets[None, :]).reshape(
        angles * PT_DEV * HITS
    )
    cosine_table, sine_table = dft_tables(PROBE)
    gathered = lax.all_gather(object_field, "strip", axis=1, tiled=True)
    full_grad = intersection_gradient(
        measured[0], positions[0], gathered[0], probe_field, cosine_table, sine_table
    )
    intersection = lax.psum_scatter(full_grad[None], "strip", scatter_dimension=1, tiled=True)
    volume_half = volume.astype(jnp.bfloat16).reshape(PT_DEV, TILE, 2 * NZ)
    partials = jnp.einsum(
        "pahrt,ptc->aphrc", radon_tiles, volume_half, preferred_element_type=jnp.float32
    )
    received = lax.all_to_all(partials, "ang", split_axis=0, concat_axis=0, tiled=True)
    selector = (range_ids[:, None] == targets_flat[None, :]).astype(jnp.float32)
    dense_rows = jnp.dot(
        selector, received.reshape(angles * PT_DEV * HITS, RAYS * 2 * NZ), precision=precise
    )
    projection = lax.psum_scatter(
        dense_rows.reshape(1, NDET, 2, NZ), "strip", scatter_dimension=1, tiled=True
    )
    object_next = object_field - object_step * (
        intersection + dual_field + penalty * (object_field - projection)
    )
    dual_next = dual_field + penalty * (object_next - projection)
    residual = (penalty * (projection - object_next) - dual_field).astype(jnp.bfloat16)
    gathered_rows = lax.all_gather(residual, "strip", axis=1, tiled=True)
    pick_table = (targets_flat[:, None] == range_ids[None, :]).astype(jnp.bfloat16)
    picked = jnp.dot(
        pick_table, gathered_rows.reshape(NR, RAYS * 2 * NZ), preferred_element_type=jnp.float32
    ).astype(jnp.bfloat16)
    picked = picked.reshape(angles, PT_DEV, HITS, RAYS, 2 * NZ)
    returned = lax.all_to_all(picked, "ang", split_axis=0, concat_axis=0, tiled=True)
    gradient = jnp.einsum(
        "pahrt,aphrc->ptc", radon_tiles, returned, preferred_element_type=jnp.float32
    )
    volume_next = volume - volume_step * gradient.reshape(volume.shape)
    return (object_next, dual_next, volume_next)


def solution(mesh):
    return jax.shard_map(
        body,
        mesh=mesh,
        in_specs=(
            P("ang", "strip", None, None),
            P("ang", "strip"),
            P(),
            P("ang", "strip", None, None),
            P("ang", "strip", None, None),
            P(("ang", "strip"), None, None),
            P(("ang", "strip"), None, None, None, None),
            P("ang", None, "strip", None),
        ),
        out_specs=(
            P("ang", "strip", None, None),
            P("ang", "strip", None, None),
            P(("ang", "strip"), None, None),
        ),
        check_vma=False,
    )
```

profile of v0, /device:TPU:0, one launch (start us, length us, event | category | flops | bytes accessed | tf_op | source)
XLA Modules:
  0.0 141.5 jit_solution(10773542326659857658)
XLA Ops:
  7.2 1.1 convert_element_type.45
  8.3 0.1 reshape.108
  8.4 1.3 convolution_bitcast_fusion
  9.7 7.5 %all-to-all-start = ((f32[16,1,2,32,256]{4,3,2,1,0:T(8,128)}), f32[16,1,2,32,256]{4,3,2,1,0:T(8,128)S(1)}, u32[]{:S(2)}, u32[]{:S(2)}) async-start(f32[16,1,2,32,256]{4,3,2,1,0:T(8,128)} %convolution_bitcast_fusion), calls=%async_computation | async-start | bytes 2097152 | tf_op jit(solution)/shard_map/all_to_all | solution.py:95
  17.3 0.9 copy-done.1
  18.2 9.4 %all_gather.6 = f32[1,512,2,128]{3,2,0,1:T(2,128)S(1)} all-gather(f32[1,256,2,128]{3,2,0,1:T(2,128)S(1)} %bitcast.213), channel_id=1, replica_groups=mesh['ang'=16,'strip'=2] {'strip'}, dimensions={1}, use_global_device_ids=true | all-gather | bytes 786432 | tf_op jit(solution)/shard_map/all_gather | solution.py:86
  27.6 1.7 %gather_fusion = f32[8,128,2,128]{3,2,1,0:T(2,128)S(1)} fusion(f32[512,2,128]{2,1,0:T(2,128)S(1)} %bitcast.206, s32[8]{0:T(128)S(1)} %fusion.61), kind=kCustom, calls=%fused_computation | custom fusion | bytes 2097248 | tf_op jit(solution)/shard_map/vmap()/gather | solution.py:52
  29.2 1.0 fusion.143
  30.3 1.2 fusion.27
  31.5 1.2 fusion.26
  32.7 1.2 fusion.8
  33.9 1.2 fusion.9
  35.1 1.1 fusion.50
  36.2 1.1 fusion.47
  37.4 1.1 convolution_add_fusion
  38.5 1.3 fusion.16
  39.9 1.3 fusion.45
  41.2 1.1 fusion.41
  42.3 1.1 fusion.7
  43.5 1.1 fusion.5
  44.6 1.1 fusion.39
  45.7 1.1 fusion.43
  46.9 1.1 fusion.2
  48.0 1.1 add_bitcast_fusion
  49.2 0.1 broadcast_in_dim.4
  49.4 21.9 %while.13 = (s32[]{:T(128)}, f32[512,2,128]{2,1,0:T(2,128)S(1)}, s32[8]{0:T(128)S(1)}, f32[8,128,2,128]{3,1,0,2:T(8,128)S(1)}, s32[]{:T(128)}, /*index=5*/s32[]{:T(128)}, s32[]{:T(128)}) while((s32[]{:T(128)}, f32[512,2,128]{2,1,0:T(2,128)S(1)}, s32[8]{0:T(128)S(1)}, f32[8,128,2,128]{3,1,0,2:T(8,128)S(1)}, s32[]{:T(128)}, ...), condition=%wide.region_1.2_spmd, body=%wide.region_0.1_spmd.sunk | while | flops 32773 | bytes 655491 | solution.py:73
  49.4 0.6 dynamic_slice.29
  52.0 0.2 fusion.162
  52.1 0.6 dynamic_slice.29
  54.7 0.2 fusion.162
  54.9 0.6 dynamic_slice.29
  57.4 0.2 fusion.162
  57.6 0.6 dynamic_slice.29
  60.2 0.2 fusion.162
  60.3 0.6 dynamic_slice.29
  62.9 0.2 fusion.162
  63.1 0.6 dynamic_slice.29
  65.6 0.2 fusion.162
  65.8 0.6 dynamic_slice.29
  68.4 0.2 fusion.162
  68.5 0.6 dynamic_slice.29
  71.1 0.2 fusion.162
  71.3 0.9 copy.122
  72.2 0.3 reduce-scatter.11.cloned.1.call-start
  72.4 0.4 copy-done.6
  73.0 0.6 copy.107
  73.6 0.5 fusion.57
  74.1 0.4 reshape.96
  74.5 0.8 copy.121
  75.4 12.6 %reduce-scatter.9.cloned.1.call-done = f32[256,256]{1,0:T(8,128)} async-done(((f32[512,256]{1,0:T(8,128)}), f32[256,256]{1,0:T(8,128)}) %reduce-scatter.9.cloned.1.call-update) | async-done | bytes 262160
  88.0 1.1 reshape.113
  89.1 15.8 %reduce-scatter.11.cloned.1.call-done = f32[256,256]{1,0:T(8,128)} async-done(((f32[512,256]{1,0:T(8,128)}), f32[256,256]{1,0:T(8,128)}) %reduce-scatter.11.cloned.1.call-update) | async-done | bytes 262160
  104.9 1.1 reshape.115
  106.0 0.3 fusion.24
  106.3 5.7 %all_gather.7 = bf16[1,512,2,128]{3,2,0,1:T(2,128)(2,1)S(1)} all-gather(bf16[1,256,2,128]{3,2,0,1:T(2,128)(2,1)S(1)} %get-tuple-element.112), channel_id=1, replica_groups=mesh['ang'=16,'strip'=2] {'strip'}, dimensions={1}, use_global_device_ids=true | all-gather | bytes 393216 | tf_op jit(solution)/shard_map/all_gather | solution.py:108
  112.0 0.2 reshape.97
  112.2 0.3 convolution_convert_fusion
  112.6 0.9 copy.109
  113.5 5.7 %all-to-all-start.1 = ((bf16[16,1,2,32,256]{4,3,2,1,0:T(8,128)(2,1)}), bf16[16,1,2,32,256]{4,3,2,1,0:T(8,128)(2,1)S(1)}, u32[]{:S(2)}, u32[]{:S(2)}) async-start(bf16[16,1,2,32,256]{4,3,2,1,0:T(8,128)(2,1)} %bitcast.28), calls=%async_computation.1 | async-start | bytes 1048576 | tf_op jit(solution)/shard_map/all_to_all | solution.py:114
  119.2 0.1 copy.78
  119.4 0.9 fusion.21
  120.3 13.2 %all-to-all-done.1 = bf16[16,1,2,32,256]{4,3,2,1,0:T(8,128)(2,1)S(1)} async-done(((bf16[16,1,2,32,256]{4,3,2,1,0:T(8,128)(2,1)}), bf16[16,1,2,32,256]{4,3,2,1,0:T(8,128)(2,1)S(1)}, u32[]{:S(2)}, u32[]{:S(2)}) %all-to-all-start.1) | async-done | bytes 524320 | tf_op jit(solution)/shard_map/all_to_all | solution.py:114
  133.5 0.3 fusion.10
  133.8 0.8 copy.79
  (33 shorter events, 0.5 us)
Async XLA Ops:
  7.2 1.2 copy-start
  9.7 7.6 %copy-start.5 = (f32[2,128,128]{2,1,0:T(8,128)S(1)}, f32[2,128,128]{2,1,0:T(8,128)}, u32[]{:S(2)}) copy-start(f32[2,128,128]{2,1,0:T(8,128)} %param.12) | copy-start | bytes 393220
  9.7 63.3 %all-to-all-start = ((f32[16,1,2,32,256]{4,3,2,1,0:T(8,128)}), f32[16,1,2,32,256]{4,3,2,1,0:T(8,128)S(1)}, u32[]{:S(2)}, u32[]{:S(2)}) async-start(f32[16,1,2,32,256]{4,3,2,1,0:T(8,128)} %convolution_bitcast_fusion), calls=%async_computation | async-start | bytes 2097152 | tf_op jit(solution)/shard_map/all_to_all | solution.py:95
  17.2 1.0 copy-start.1
  17.2 70.8 %reduce-scatter.9.cloned.1.call-start = ((), (), s32[]{:S(2)}) async-start(), calls=%async_computation.4 | async-start | bytes 786432
  18.2 9.4 %copy-start.8 = (s32[1,8]{1,0:T(1,128)S(1)}, s32[1,8]{1,0:T(1,128)}, u32[]{:S(2)}) copy-start(s32[1,8]{1,0:T(1,128)} %param.11) | copy-start | bytes 100
  37.4 1.2 copy-start.7
  72.1 0.7 copy-start.6
  72.2 32.7 %reduce-scatter.11.cloned.1.call-start = ((), (), s32[]{:S(2)}) async-start(), calls=%async_computation.5 | async-start | bytes 786432
  89.1 16.9 %copy-start.3 = (f32[1,256,2,128]{3,2,1,0:T(2,128)S(1)}, f32[1,256,2,128]{3,2,1,0:T(2,128)}, u32[]{:S(2)}) copy-start(f32[1,256,2,128]{3,2,1,0:T(2,128)} %param.14) | copy-start | bytes 786436
  106.3 13.1 %copy-start.4 = (f32[1,256,2,128]{3,2,1,0:T(2,128)}, f32[1,256,2,128]{3,2,1,0:T(2,128)S(1)}, u32[]{:S(2)}) copy-start(f32[1,256,2,128]{3,2,1,0:T(2,128)S(1)} %get-tuple-element.113) | copy-start | bytes 786436
  113.5 5.7 %copy-start.2 = (f32[256,2,128]{2,1,0:T(2,128)S(1)}, f32[256,2,128]{2,1,0:T(2,128)}, u32[]{:S(2)}) copy-start(f32[256,2,128]{2,1,0:T(2,128)} %param.15) | copy-start | bytes 786436
  113.5 20.0 %all-to-all-start.1 = ((bf16[16,1,2,32,256]{4,3,2,1,0:T(8,128)(2,1)}), bf16[16,1,2,32,256]{4,3,2,1,0:T(8,128)(2,1)S(1)}, u32[]{:S(2)}, u32[]{:S(2)}) async-start(bf16[16,1,2,32,256]{4,3,2,1,0:T(8,128)(2,1)} %bitcast.28), calls=%async_computation.1 | async-start | bytes 1048576 | tf_op jit(solution)/shard_map/all_to_all | solution.py:114
Sparse Core Ops, SparseCore 0:
  72.3 15.6 reduce-scatter.8
  90.2 14.6 reduce-scatter.10
where the time goes:
time: 142 us
  waiting for transfers between devices  41.6 us (29%)
  matrix products  21.2 us (15%)
  local copies, waits for them, and re-layouts  16.1 us (11%)
  loops' own time  15.7 us (11%)
  blocking collectives  15.1 us (11%)
  between operations  14.4 us (10%)
  starting transfers between devices  13.5 us (10%)
  other arithmetic  3.78 us (3%)
    unnamed x4, waiting for transfers between devices  28.4 us
    another operation x1, loops' own time, intersection_gradient(): lax.fori_loop(0, starts.shape[0], deposit, jnp.zeros(field.shape, jnp.flo...  15.7 us
    all_to_all x1, waiting for transfers between devices, body(): lax.all_to_all(picked, 'ang', split_axis=0, concat_axis=0, tiled=True)  13.2 us
    all_gather x1, blocking collectives, body(): gathered = lax.all_gather(object_field, 'strip', axis=1, tiled=True)  9.4 us
    unnamed x26, local copies, waits for them, and re-layouts  7.64 us
    all_to_all x1, starting transfers between devices, body(): lax.all_to_all(partials, 'ang', split_axis=0, concat_axis=0, tiled=True)  7.52 us
    all_gather x1, blocking collectives, body(): gathered_rows = lax.all_gather(residual, 'strip', axis=1, tiled=True)  5.75 us
    all_to_all x1, starting transfers between devices, body(): lax.all_to_all(picked, 'ang', split_axis=0, concat_axis=0, tiled=True)  5.73 us
  transfers between devices with their start and end apart: 4, of which 3 were waited for; matrix products, arithmetic and copies ran while one was open for 24% of the time, Pallas kernels for 0%

commit v1 on v0

v1 whole, which is shorter than its diff:
```python
import functools
import math

import jax
import jax.numpy as jnp
import numpy as np
from jax import lax
from jax.experimental import pallas as pl
from jax.experimental.pallas import tpu as pltpu
from jax.sharding import PartitionSpec as P

RAYS = 32

penalty = 1.0
object_step = 0.1
volume_step = 1.0
MESH = pl.DeviceIdType.MESH


def dft_tables(length):
    indices = np.arange(length, dtype=np.int64)
    angles = (indices[:, None] * indices[None, :] % length) * (2.0 * math.pi / length)
    scaling = 1.0 / math.sqrt(length)
    parts = []
    for table in (np.cos(angles) * scaling, np.sin(angles) * scaling):
        table = table.astype(np.float32)
        high = table.astype(jnp.bfloat16)
        parts += [high, (table - high.astype(np.float32)).astype(jnp.bfloat16)]
    return np.stack(parts)


def split(value):
    high = value.astype(jnp.bfloat16)
    return high, (value - high.astype(jnp.float32)).astype(jnp.bfloat16)


def dot(left, right):
    return jnp.dot(left, right, preferred_element_type=jnp.float32)


def dot3(left, right):
    return dot(left[0], right[0]) + (dot(left[0], right[1]) + dot(left[1], right[0]))


def beside(left, right):
    return jnp.concatenate([left, right], axis=1)


def above(top, low):
    return jnp.concatenate([top, low], axis=0)


def swap_blocks(value):
    half = value.shape[1] // 2
    return above(
        beside(value[:half, :half], value[half:, :half]),
        beside(value[:half, half:], value[half:, half:]),
    )


def both_parts(ref, columns):
    return beside(ref[pl.ds(0, columns, stride=2), :], ref[pl.ds(1, columns, stride=2), :])


def put_parts(ref, value):
    columns, half = value.shape[0], value.shape[1] // 2
    ref[pl.ds(0, columns, stride=2), :] = value[:, :half]
    ref[pl.ds(1, columns, stride=2), :] = value[:, half:]


def window(start, count, rows):
    first = lax.broadcasted_iota(jnp.int32, (count, rows), 0) + start
    return one_where(first == lax.broadcasted_iota(jnp.int32, (count, rows), 1))


def one_where(mask):
    return jnp.where(mask, 1.0, 0.0).astype(jnp.bfloat16)


def one_hot(rows, starts, count, width, scale):
    lanes = lax.broadcasted_iota(jnp.int32, (1, count * width), 1)
    block = lanes // width
    target = lanes % width
    for k in range(count):
        target = target + jnp.where(block == k, starts[k] * scale, 0)
    row = lax.broadcasted_iota(jnp.int32, (rows, count * width), 0)
    return one_where(row == target)


def kernel(
    angles, strips, order,
    positions, ranges, measured, probe, field, dual, volume, radon, tables,
    object_next, dual_next, volume_next,
    ray_out, ray_in, pick_out, pick_in, field_out, field_in, grad_out, grad_in,
    dense_out, dense_in, rows_half, whole_field, grads, total_grad, total_rays, gathered_radon, picker,
    ray_send, ray_recv, pick_send, pick_recv, strip_send, strip_recv,
):
    me, strip = lax.axis_index("ang"), lax.axis_index("strip")
    columns = field.shape[0] // 2
    detector = strips * columns
    frames, side = measured.shape[0], measured.shape[1]
    hit_rows = ray_out.shape[1]
    ang_peers = [lax.rem(me + offset, angles) for offset in order]
    strip_peers = [lax.rem(strip + offset, strips) for offset in range(1, strips)]
    own = pl.ds(pl.multiple_of(strip * columns, columns), columns)

    barrier = pltpu.get_barrier_semaphore()
    for peer in ang_peers:
        pl.semaphore_signal(barrier, inc=1, device_id=(peer, strip), device_id_type=MESH)
    for peer in strip_peers:
        pl.semaphore_signal(barrier, inc=1, device_id=(me, peer), device_id_type=MESH)

    own_field = both_parts(field, columns)
    field_out[...] = own_field.astype(jnp.bfloat16)
    volume_half = both_parts(volume, volume.shape[0] // 2).astype(jnp.bfloat16)
    sums = dot(radon[...], volume_half).astype(jnp.bfloat16)
    ray_out[...] = sums.reshape(ray_out.shape)
    pl.semaphore_wait(barrier, len(ang_peers) + len(strip_peers))

    def strip_copy(source, target, stage, slot, peer):
        return pltpu.make_async_remote_copy(
            src_ref=source, dst_ref=target,
            send_sem=strip_send.at[stage, peer], recv_sem=strip_recv.at[stage, slot],
            device_id=(me, peer), device_id_type=MESH,
        )

    def ang_copy(source, target, send, recv, slot, peer):
        return pltpu.make_async_remote_copy(
            src_ref=source, dst_ref=target, send_sem=send.at[peer], recv_sem=recv.at[slot],
            device_id=(peer, strip), device_id_type=MESH,
        )

    started = []

    def start(copy):
        copy.start()
        started.append(copy)

    for peer in strip_peers:
        start(strip_copy(field_out, field_in.at[strip], 0, strip, peer))
    for peer in ang_peers:
        start(ang_copy(ray_out.at[peer], ray_in.at[me], ray_send, ray_recv, me, peer))
    ray_in[me] = ray_out[me]

    gathered_radon[...] = radon[...].T
    cos_high, cos_low, sin_high, sin_low = (tables[k] for k in range(4))
    turn = tuple(
        above(beside(c, -s), beside(s, c)) for c, s in ((cos_high, sin_high), (cos_low, sin_low))
    )
    back_turn = tuple(
        above(beside(c, s), beside(-s, c)) for c, s in ((cos_high, sin_high), (cos_low, sin_low))
    )
    probe_re, probe_im = probe[0], probe[1]
    whole_field[own, :] = own_field
    for peer in strip_peers:
        strip_copy(field_out, field_in.at[peer], 0, peer, peer).wait_recv()
        rows = pl.ds(pl.multiple_of(peer * columns, columns), columns)
        whole_field[rows, :] = field_in[peer].astype(jnp.float32)

    field_high, field_low = split(whole_field[...])
    for pair in range(0, frames, 2):
        waves = []
        for j in (pair, pair + 1):
            cut = window(positions[j], side, detector)
            patch = dot(cut, field_high) + dot(cut, field_low)
            re, im = patch[:, :side], patch[:, side:]
            waves.append(beside(probe_re * re - probe_im * im, probe_re * im + probe_im * re))
        right = dot3(split(above(*waves)), turn)
        far = dot3(back_turn, split(swap_blocks(right)))
        far_re, far_im = far[:side], far[side:]
        modulus = jnp.sqrt(far_re * far_re + far_im * far_im)
        intensity = beside(measured[pair], measured[pair + 1])
        shrink = 1.0 - jnp.sqrt(intensity) / jnp.maximum(modulus, 1.0)
        left = dot3(turn, split(above(far_re * shrink, far_im * shrink)))
        back = dot3(split(swap_blocks(left)), back_turn)
        for k in range(2):
            part = back[k * side:(k + 1) * side]
            re, im = part[:, :side], part[:, side:]
            grads[(pair + k) * side:(pair + k + 1) * side, :] = beside(
                probe_re * re + probe_im * im, probe_re * im - probe_im * re
            )
    deposit = one_hot(detector, [positions[j] for j in range(frames)], frames, side, 1)
    high, low = split(grads[...])
    total_grad[...] = dot(deposit, high) + dot(deposit, low)
    for k in range(strips):
        grad_out[k] = total_grad[k * columns:(k + 1) * columns, :].astype(jnp.bfloat16)
    for peer in strip_peers:
        start(strip_copy(grad_out.at[peer], grad_in.at[strip], 1, strip, peer))

    selector = one_hot(
        detector, [ranges[k] for k in range(angles)], angles, hit_rows, RAYS
    )
    for k in range(angles):
        picker[k] = window(ranges[k] * RAYS, hit_rows, detector)
    for peer in ang_peers:
        ang_copy(ray_out.at[peer], ray_in.at[peer], ray_send, ray_recv, peer, peer).wait_recv()
    total_rays[...] = dot(selector, ray_in[...].reshape(angles * hit_rows, ray_in.shape[2]))
    for k in range(strips):
        dense_out[k] = total_rays[k * columns:(k + 1) * columns, :].astype(jnp.bfloat16)
    for peer in strip_peers:
        start(strip_copy(dense_out.at[peer], dense_in.at[strip], 2, strip, peer))

    intersection = total_grad[own, :]
    for peer in strip_peers:
        strip_copy(grad_out.at[peer], grad_in.at[peer], 1, peer, peer).wait_recv()
        intersection = intersection + grad_in[peer].astype(jnp.float32)
    projection = total_rays[own, :]
    for peer in strip_peers:
        strip_copy(dense_out.at[peer], dense_in.at[peer], 2, peer, peer).wait_recv()
        projection = projection + dense_in[peer].astype(jnp.float32)
    own_dual = both_parts(dual, columns)
    own_field = whole_field[own, :]
    updated = own_field - object_step * (
        intersection + own_dual + penalty * (own_field - projection)
    )
    residual = penalty * (projection - updated) - own_dual
    rows_half[own, :] = residual.astype(jnp.bfloat16)
    for peer in strip_peers:
        start(strip_copy(rows_half.at[own], rows_half.at[own], 3, strip, peer))
    put_parts(object_next, updated)
    put_parts(dual_next, own_dual + penalty * (updated - projection))
    for peer in strip_peers:
        rows = pl.ds(pl.multiple_of(peer * columns, columns), columns)
        strip_copy(rows_half.at[rows], rows_half.at[rows], 3, peer, peer).wait_recv()

    rows = rows_half[...]
    for peer in ang_peers:
        pick_out[peer] = dot(picker[peer], rows).astype(jnp.bfloat16)
        start(ang_copy(pick_out.at[peer], pick_in.at[me], pick_send, pick_recv, me, peer))
    pick_in[me] = dot(picker[me], rows).astype(jnp.bfloat16)
    own_volume = both_parts(volume, volume.shape[0] // 2)
    for peer in ang_peers:
        ang_copy(pick_out.at[peer], pick_in.at[peer], pick_send, pick_recv, peer, peer).wait_recv()
    gradient = dot(
        gathered_radon[...], pick_in[...].reshape(angles * hit_rows, pick_in.shape[2])
    )
    put_parts(volume_next, own_volume - volume_step * gradient)
    for copy in started:
        copy.wait_send()


def body(
    measured, positions, probe_field, object_field, dual_field, volume, radon_tiles, tile_range
):
    angles, strips = lax.axis_size("ang"), lax.axis_size("strip")
    order = sorted(range(1, angles), key=lambda offset: abs(offset - angles // 2))
    frames, side = measured.shape[1], measured.shape[2]
    columns, width = object_field.shape[1], object_field.shape[2] * object_field.shape[3]
    hit_rows = radon_tiles.shape[2] * radon_tiles.shape[3]
    pixels = radon_tiles.shape[4]
    slices = object_field.shape[3]
    vmem = pl.BlockSpec(memory_space=pltpu.VMEM)
    smem = pl.BlockSpec(memory_space=pltpu.SMEM)
    half = jnp.bfloat16
    outs = pl.pallas_call(
        functools.partial(kernel, angles, strips, order),
        out_shape=(
            jax.ShapeDtypeStruct((2 * columns, slices), jnp.float32),
            jax.ShapeDtypeStruct((2 * columns, slices), jnp.float32),
            jax.ShapeDtypeStruct((2 * pixels, slices), jnp.float32),
        ),
        in_specs=[smem, smem] + [vmem] * 7,
        out_specs=(vmem, vmem, vmem),
        scratch_shapes=[
            pltpu.VMEM((angles, hit_rows, width), half),
            pltpu.VMEM((angles, hit_rows, width), half),
            pltpu.VMEM((angles, hit_rows, width), half),
            pltpu.VMEM((angles, hit_rows, width), half),
            pltpu.VMEM((columns, width), half),
            pltpu.VMEM((strips, columns, width), half),
            pltpu.VMEM((strips, columns, width), half),
            pltpu.VMEM((strips, columns, width), half),
            pltpu.VMEM((strips, columns, width), half),
            pltpu.VMEM((strips, columns, width), half),
            pltpu.VMEM((strips * columns, width), half),
            pltpu.VMEM((strips * columns, width), jnp.float32),
            pltpu.VMEM((frames * side, width), jnp.float32),
            pltpu.VMEM((strips * columns, width), jnp.float32),
            pltpu.VMEM((strips * columns, width), jnp.float32),
            pltpu.VMEM((pixels, angles * hit_rows), half),
            pltpu.VMEM((angles, hit_rows, strips * columns), half),
            pltpu.SemaphoreType.DMA((angles,)),
            pltpu.SemaphoreType.DMA((angles,)),
            pltpu.SemaphoreType.DMA((angles,)),
            pltpu.SemaphoreType.DMA((angles,)),
            pltpu.SemaphoreType.DMA((4, strips)),
            pltpu.SemaphoreType.DMA((4, strips)),
        ],
        compiler_params=pltpu.CompilerParams(
            collective_id=0, has_side_effects=True, vmem_limit_bytes=48 * 1024 * 1024
        ),
    )(
        positions.reshape(frames),
        tile_range.reshape(angles),
        measured[0],
        probe_field,
        object_field.reshape(2 * columns, slices),
        dual_field.reshape(2 * columns, slices),
        volume.reshape(2 * pixels, slices),
        radon_tiles.reshape(angles * hit_rows, pixels),
        jnp.asarray(dft_tables(side)),
    )
    return (
        outs[0].reshape(object_field.shape),
        outs[1].reshape(dual_field.shape),
        outs[2].reshape(volume.shape),
    )


def solution(mesh):
    return jax.shard_map(
        body,
        mesh=mesh,
        in_specs=(
            P("ang", "strip", None, None),
            P("ang", "strip"),
            P(),
            P("ang", "strip", None, None),
            P("ang", "strip", None, None),
            P(("ang", "strip"), None, None),
            P(("ang", "strip"), None, None, None, None),
            P("ang", None, "strip", None),
        ),
        out_specs=(
            P("ang", "strip", None, None),
            P("ang", "strip", None, None),
            P(("ang", "strip"), None, None),
        ),
        check_vma=False,
    )
```

time: 142 us -> 52.5 us (0.37)
  Pallas kernels: 0 us -> 42 us
  waiting for transfers between devices: 41.6 us -> 0 us
  matrix products: 21.2 us -> 0 us
  loops' own time: 15.7 us -> 0 us
  blocking collectives: 15.1 us -> 0 us
  between operations: 14.4 us -> 0.67 us
  starting transfers between devices: 13.5 us -> 0 us
  local copies, waits for them, and re-layouts: 16.1 us -> 9.5 us
  other arithmetic: 3.78 us -> 0 us
    pallas_call x0 -> x1, Pallas kernels: none -> 42 us  [body(): pl.pallas_call(functools.partial(kernel, angles, strips, order), out_shap...]
    unnamed x4 -> x0, waiting for transfers between devices: 28.4 us -> none
    dot_general x20 -> x0, matrix products: 21.2 us -> none  [the longest x2 2.5 us: transform(): jnp.einsum('fkr,rl->fkl', left_re, sine_table, precision=precise)]
    another operation x1 -> x0, loops' own time: 15.7 us -> none  [intersection_gradient(): lax.fori_loop(0, starts.shape[0], deposit, jnp.zeros(field.shape, jnp.flo...]
    all_gather x2 -> x0, blocking collectives: 15.1 us -> none  [the longest x1 9.4 us: body(): gathered = lax.all_gather(object_field, 'strip', axis=1, tiled=True)]
    all_to_all x2 -> x0, starting transfers between devices: 13.2 us -> none  [the longest x1 7.52 us: body(): lax.all_to_all(partials, 'ang', split_axis=0, concat_axis=0, tiled=True)]
    all_to_all x2 -> x0, waiting for transfers between devices: 13.2 us -> none  [the longest x1 13.2 us: body(): lax.all_to_all(picked, 'ang', split_axis=0, concat_axis=0, tiled=True)]
    dynamic_slice x16 -> x0, local copies, waits for them, and re-layouts: 4.83 us -> none  [the longest x8 4.69 us: deposit(): piece = lax.dynamic_slice_in_dim(total, starts[index], window, 0)]
  transfers between devices with their start and end apart: 4 -> 0, of which waited for: 3 -> 0; matrix products, arithmetic and copies ran while one was open for 24% -> 0% of each run, Pallas kernels for 0% -> 0%
where the time goes in v1:
time: 52.5 us; the launch traced here: 52.1 us
  Pallas kernels  42 us (80%)
  local copies, waits for them, and re-layouts  9.5 us (18%)
  between operations  0.67 us (1%)
    pallas_call x1, Pallas kernels, body(): pl.pallas_call(functools.partial(kernel, angles, strips, order), out_shap...  42 us
    unnamed x21, local copies, waits for them, and re-layouts  9.5 us

profile of v1, /device:TPU:0, one launch (start us, length us, event | category | flops | bytes accessed | tf_op | source)
XLA Modules:
  0.0 52.1 jit_solution(5829952823631610924)
XLA Ops:
  0.6 0.0 copy-start.7
  0.6 0.0 copy-start.8
  0.7 0.6 %copy-done.7 = s32[1,8]{1,0:T(1,128)S(1)} copy-done((s32[1,8]{1,0:T(1,128)S(1)}, s32[1,8]{1,0:T(1,128)}, u32[]{:S(2)}) %copy-start.7) | copy-done | bytes 56
  1.3 0.0 copy-done.8
  1.3 0.0 copy-start
  1.3 1.0 %copy-done = f32[1,8,128,128]{3,2,1,0:T(8,128)S(1)} copy-done((f32[1,8,128,128]{3,2,1,0:T(8,128)S(1)}, f32[1,8,128,128]{3,2,1,0:T(8,128)}, u32[]{:S(2)}) %copy-start) | copy-done | bytes 524312
  2.3 0.0 copy-start.1
  2.3 1.0 %copy-done.1 = bf16[1,16,2,32,256]{4,3,2,1,0:T(8,128)(2,1)S(1)} copy-done((bf16[1,16,2,32,256]{4,3,2,1,0:T(8,128)(2,1)S(1)}, bf16[1,16,2,32,256]{4,3,2,1,0:T(8,128)(2,1)}, u32[]{:S(2)}) %copy-start.1) | copy-done | bytes 524312
  3.4 0.0 copy-start.2
  3.4 0.9 %copy-done.2 = f32[1,256,2,128]{3,2,1,0:T(2,128)S(1)} copy-done((f32[1,256,2,128]{3,2,1,0:T(2,128)S(1)}, f32[1,256,2,128]{3,2,1,0:T(2,128)}, u32[]{:S(2)}) %copy-start.2) | copy-done | bytes 262168
  4.3 0.0 copy-start.3
  4.3 0.9 %copy-done.3 = f32[1,256,2,128]{3,2,1,0:T(2,128)S(1)} copy-done((f32[1,256,2,128]{3,2,1,0:T(2,128)S(1)}, f32[1,256,2,128]{3,2,1,0:T(2,128)}, u32[]{:S(2)}) %copy-start.3) | copy-done | bytes 262168
  5.3 0.0 copy-start.4
  5.3 0.9 %copy-done.4 = f32[256,2,128]{2,1,0:T(2,128)S(1)} copy-done((f32[256,2,128]{2,1,0:T(2,128)S(1)}, f32[256,2,128]{2,1,0:T(2,128)}, u32[]{:S(2)}) %copy-start.4) | copy-done | bytes 262168
  6.2 0.0 copy-start.5
  6.2 0.9 %copy-done.5 = f32[2,128,128]{2,1,0:T(8,128)S(1)} copy-done((f32[2,128,128]{2,1,0:T(8,128)S(1)}, f32[2,128,128]{2,1,0:T(8,128)}, u32[]{:S(2)}) %copy-start.5) | copy-done | bytes 131096
  7.1 0.0 copy-start.6
  7.1 0.9 %copy-done.6 = bf16[4,128,128]{2,1,0:T(8,128)(2,1)S(1)} copy-done((bf16[4,128,128]{2,1,0:T(8,128)(2,1)S(1)}, bf16[4,128,128]{2,1,0:T(8,128)(2,1)}, u32[]{:S(2)}) %copy-start.6) | copy-done | bytes 131096
  8.1 42.0 %shard_map.112 = (f32[512,128]{1,0:T(8,128)S(1)}, f32[512,128]{1,0:T(8,128)S(1)}, f32[512,128]{1,0:T(8,128)S(1)}) custom-call(s32[8]{0:T(128)S(1)} %bitcast.18, s32[16]{0:T(128)S(1)} %bitcast.19, f32[8,128,128]{2,1,0:T(8,128)S(1)} %bitcast.10, f32[2,128,128]{2,1,0:T(8,128)S(1)} %copy-done.5, f32[512,128]{1,0:T(8,128)S(1)} %bitcast.15, ...), custom_call_target="tpu_custom_call" | custom-call | tf_op jit(solution)/shard_map/pallas_call | solution.py:255
  50.0 0.7 %copy.15 = f32[1,256,2,128]{3,2,1,0:T(2,128)} copy(f32[1,256,2,128]{3,2,1,0:T(2,128)S(1)} %bitcast.14) | data formatting | bytes 524288
  50.7 0.7 %copy.16 = f32[1,256,2,128]{3,2,1,0:T(2,128)} copy(f32[1,256,2,128]{3,2,1,0:T(2,128)S(1)} %bitcast.13) | data formatting | bytes 524288
  51.4 0.7 %copy.17 = f32[256,2,128]{2,1,0:T(2,128)} copy(f32[256,2,128]{2,1,0:T(2,128)S(1)} %bitcast.12) | data formatting | bytes 524288
Async XLA Ops:
  0.6 0.7 %copy-start.7 = (s32[1,8]{1,0:T(1,128)S(1)}, s32[1,8]{1,0:T(1,128)}, u32[]{:S(2)}) copy-start(s32[1,8]{1,0:T(1,128)} %param.10) | copy-start | bytes 100
  0.6 0.7 %copy-start.8 = (s32[1,16,1,1]{1,3,2,0:T(1,128)S(1)}, s32[1,16,1,1]{1,3,2,0:T(1,128)}, u32[]{:S(2)}) copy-start(s32[1,16,1,1]{1,3,2,0:T(1,128)} %param.16) | copy-start | bytes 196
  1.3 1.0 %copy-start = (f32[1,8,128,128]{3,2,1,0:T(8,128)S(1)}, f32[1,8,128,128]{3,2,1,0:T(8,128)}, u32[]{:S(2)}) copy-start(f32[1,8,128,128]{3,2,1,0:T(8,128)} %param.9) | copy-start | bytes 1572868
  2.3 1.0 %copy-start.1 = (bf16[1,16,2,32,256]{4,3,2,1,0:T(8,128)(2,1)S(1)}, bf16[1,16,2,32,256]{4,3,2,1,0:T(8,128)(2,1)}, u32[]{:S(2)}) copy-start(bf16[1,16,2,32,256]{4,3,2,1,0:T(8,128)(2,1)} %param.15) | copy-start | bytes 1572868
  3.4 0.9 %copy-start.2 = (f32[1,256,2,128]{3,2,1,0:T(2,128)S(1)}, f32[1,256,2,128]{3,2,1,0:T(2,128)}, u32[]{:S(2)}) copy-start(f32[1,256,2,128]{3,2,1,0:T(2,128)} %param.12) | copy-start | bytes 786436
  4.3 0.9 %copy-start.3 = (f32[1,256,2,128]{3,2,1,0:T(2,128)S(1)}, f32[1,256,2,128]{3,2,1,0:T(2,128)}, u32[]{:S(2)}) copy-start(f32[1,256,2,128]{3,2,1,0:T(2,128)} %param.13) | copy-start | bytes 786436
  5.3 0.9 %copy-start.4 = (f32[256,2,128]{2,1,0:T(2,128)S(1)}, f32[256,2,128]{2,1,0:T(2,128)}, u32[]{:S(2)}) copy-start(f32[256,2,128]{2,1,0:T(2,128)} %param.14) | copy-start | bytes 786436
  6.2 0.9 %copy-start.5 = (f32[2,128,128]{2,1,0:T(8,128)S(1)}, f32[2,128,128]{2,1,0:T(8,128)}, u32[]{:S(2)}) copy-start(f32[2,128,128]{2,1,0:T(8,128)} %probe.1) | copy-start | bytes 393220
  7.1 0.9 %copy-start.6 = (bf16[4,128,128]{2,1,0:T(8,128)(2,1)S(1)}, bf16[4,128,128]{2,1,0:T(8,128)(2,1)}, u32[]{:S(2)}) copy-start(bf16[4,128,128]{2,1,0:T(8,128)(2,1)} %constant.2.clone.tables) | copy-start | bytes 393220

commit v2 on v1

v2 whole, which is shorter than its diff:
```python
import functools
import math

import jax
import jax.numpy as jnp
import numpy as np
from jax import lax
from jax.experimental import pallas as pl
from jax.experimental.pallas import tpu as pltpu
from jax.sharding import PartitionSpec as P

RAYS = 32
VMEM_BYTES = 67043328

penalty = 1.0
object_step = 0.1
volume_step = 1.0
MESH = pl.DeviceIdType.MESH


def dft_tables(length):
    indices = np.arange(length, dtype=np.int64)
    angles = (indices[:, None] * indices[None, :] % length) * (2.0 * math.pi / length)
    scaling = 1.0 / math.sqrt(length)
    parts = []
    for table in (np.cos(angles) * scaling, np.sin(angles) * scaling):
        table = table.astype(np.float32)
        high = table.astype(jnp.bfloat16)
        parts += [high, (table - high.astype(np.float32)).astype(jnp.bfloat16)]
    return np.stack(parts)


def split(value):
    high = value.astype(jnp.bfloat16)
    return high, (value - high.astype(jnp.float32)).astype(jnp.bfloat16)


def dot(left, right):
    return jnp.dot(left, right, preferred_element_type=jnp.float32)


def dot3(left, right):
    return dot(left[0], right[0]) + (dot(left[0], right[1]) + dot(left[1], right[0]))


def beside(left, right):
    return jnp.concatenate([left, right], axis=1)


def above(top, low):
    return jnp.concatenate([top, low], axis=0)


def swap_blocks(value):
    half = value.shape[1] // 2
    return above(
        beside(value[:half, :half], value[half:, :half]),
        beside(value[:half, half:], value[half:, half:]),
    )


def both_parts(ref, columns):
    return beside(ref[pl.ds(0, columns, stride=2), :], ref[pl.ds(1, columns, stride=2), :])


def put_parts(ref, value):
    columns, half = value.shape[0], value.shape[1] // 2
    ref[pl.ds(0, columns, stride=2), :] = value[:, :half]
    ref[pl.ds(1, columns, stride=2), :] = value[:, half:]


def window(start, count, rows):
    first = lax.broadcasted_iota(jnp.int32, (count, rows), 0) + start
    return one_where(first == lax.broadcasted_iota(jnp.int32, (count, rows), 1))


def one_where(mask):
    return jnp.where(mask, 1.0, 0.0).astype(jnp.bfloat16)


def one_hot(rows, starts, count, width, scale):
    lanes = lax.broadcasted_iota(jnp.int32, (1, count * width), 1)
    block = lanes // width
    target = lanes % width
    for k in range(count):
        target = target + jnp.where(block == k, starts[k] * scale, 0)
    row = lax.broadcasted_iota(jnp.int32, (rows, count * width), 0)
    return one_where(row == target)


def xor(left, right, bound):
    result, bit = 0, 1
    while bit < bound:
        result = result + ((left // bit) + (right // bit)) % 2 * bit
        bit *= 2
    return result


def kernel(
    angles, strips,
    positions, ranges, measured_hbm, probe_hbm, field_hbm, dual_hbm, volume_hbm, radon_hbm,
    tables_hbm,
    object_next, dual_next, volume_next,
    measured, probe, field, dual, volume, radon, tables,
    ray_out, ray_in, pick_out, pick_in, field_out, field_in, grad_out, grad_in,
    dense_out, dense_in, rows_half, whole_field, grads, total_grad, total_rays, turned_radon,
    picker, selector,
    load_sem, ray_send, ray_recv, pick_send, pick_recv, strip_send, strip_recv,
):
    loads = {}
    for k, (name, source, target) in enumerate((
        ("volume", volume_hbm, volume), ("radon", radon_hbm, radon), ("field", field_hbm, field),
        ("tables", tables_hbm, tables), ("probe", probe_hbm, probe),
        ("measured", measured_hbm, measured), ("dual", dual_hbm, dual),
    )):
        loads[name] = pltpu.make_async_copy(source, target, load_sem.at[k])
        loads[name].start()
    me, strip = lax.axis_index("ang"), lax.axis_index("strip")
    columns = field.shape[0] // 2
    detector = strips * columns
    frames, side = measured.shape[0], measured.shape[1]
    slices = field.shape[1]
    chunks, hit_rows = ray_out.shape[0], ray_out.shape[2]
    if angles & (angles - 1):
        ang_peers = [lax.rem(me + offset, angles) for offset in range(1, angles)]
    else:
        ang_peers = [xor(me, offset, angles) for offset in range(angles - 1, 0, -1)]
    strip_peers = [lax.rem(strip + offset, strips) for offset in range(1, strips)]

    def rows_of(owner):
        return pl.ds(pl.multiple_of(owner * columns, columns), columns)

    barrier = pltpu.get_barrier_semaphore()
    for peer in ang_peers:
        pl.semaphore_signal(barrier, inc=1, device_id=(peer, strip), device_id_type=MESH)
    for peer in strip_peers:
        pl.semaphore_signal(barrier, inc=1, device_id=(me, peer), device_id_type=MESH)

    loads["volume"].wait()
    loads["radon"].wait()
    pixels = volume.shape[0] // 2
    volume_half = both_parts(volume, pixels).astype(jnp.bfloat16)
    sums = dot(radon[...], volume_half).astype(jnp.bfloat16)
    for c in range(chunks):
        ray_out[c] = sums[:, c * slices:(c + 1) * slices].reshape(ray_out.shape[1:])
    loads["field"].wait()
    own_field = both_parts(field, columns)
    field_out[...] = own_field.astype(jnp.bfloat16)
    pl.semaphore_wait(barrier, len(ang_peers) + len(strip_peers))

    def strip_copy(source, target, stage, slot, peer):
        return pltpu.make_async_remote_copy(
            src_ref=source, dst_ref=target,
            send_sem=strip_send.at[stage, peer], recv_sem=strip_recv.at[stage, slot],
            device_id=(me, peer), device_id_type=MESH,
        )

    def ray_copy(c, slot, peer):
        return pltpu.make_async_remote_copy(
            src_ref=ray_out.at[c, peer], dst_ref=ray_in.at[c, slot],
            send_sem=ray_send.at[c, peer], recv_sem=ray_recv.at[c, slot],
            device_id=(peer, strip), device_id_type=MESH,
        )

    def pick_copy(c, slot, peer):
        return pltpu.make_async_remote_copy(
            src_ref=pick_out.at[c, peer], dst_ref=pick_in.at[c, slot],
            send_sem=pick_send.at[c, peer], recv_sem=pick_recv.at[c, slot],
            device_id=(peer, strip), device_id_type=MESH,
        )

    def grad_copy(c, slot, peer):
        return strip_copy(grad_out.at[c, peer], grad_in.at[c, slot], 1 + c, slot, peer)

    def dense_copy(c, slot, peer):
        return strip_copy(
            dense_out.at[c, peer], dense_in.at[c, slot], 1 + chunks + c, slot, peer
        )

    def residual_copy(c, owner, peer):
        part = rows_half.at[c, rows_of(owner), :]
        return strip_copy(part, part, 1 + 2 * chunks + c, owner, peer)

    started = []

    def start(copy):
        copy.start()
        started.append(copy)

    for peer in ang_peers:
        start(ray_copy(0, me, peer))
    for peer in strip_peers:
        start(strip_copy(field_out, field_in.at[strip], 0, strip, peer))
    for c in range(1, chunks):
        for peer in ang_peers:
            start(ray_copy(c, me, peer))

    for c in range(chunks):
        ray_in[c, me] = ray_out[c, me]
    selector[...] = one_hot(
        detector, [ranges[k] for k in range(angles)], angles, hit_rows, RAYS
    )
    for name in ("tables", "probe", "measured", "dual"):
        loads[name].wait()
    cos_high, cos_low, sin_high, sin_low = (tables[k] for k in range(4))
    turn = tuple(
        above(beside(c, -s), beside(s, c)) for c, s in ((cos_high, sin_high), (cos_low, sin_low))
    )
    back_turn = tuple(
        above(beside(c, s), beside(-s, c)) for c, s in ((cos_high, sin_high), (cos_low, sin_low))
    )
    probe_re, probe_im = probe[0], probe[1]
    whole_field[rows_of(strip), :] = own_field
    for peer in strip_peers:
        strip_copy(field_out, field_in.at[peer], 0, peer, peer).wait_recv()
        whole_field[rows_of(peer), :] = field_in[peer].astype(jnp.float32)
    field_high, field_low = split(whole_field[...])

    def frame_pair(pair):
        waves = []
        for j in (pair, pair + 1):
            cut = window(positions[j], side, detector)
            patch = dot(cut, field_high) + dot(cut, field_low)
            re, im = patch[:, :side], patch[:, side:]
            waves.append(beside(probe_re * re - probe_im * im, probe_re * im + probe_im * re))
        right = dot3(split(above(*waves)), turn)
        far = dot3(back_turn, split(swap_blocks(right)))
        far_re, far_im = far[:side], far[side:]
        modulus = jnp.sqrt(far_re * far_re + far_im * far_im)
        intensity = beside(measured[pair], measured[pair + 1])
        shrink = 1.0 - jnp.sqrt(intensity) / jnp.maximum(modulus, 1.0)
        left = dot3(turn, split(above(far_re * shrink, far_im * shrink)))
        back = dot3(split(swap_blocks(left)), back_turn)
        for k in range(2):
            part = back[k * side:(k + 1) * side]
            re, im = part[:, :side], part[:, side:]
            grads[(pair + k) * side:(pair + k + 1) * side, :] = beside(
                probe_re * re + probe_im * im, probe_re * im - probe_im * re
            )

    def sum_rays(c):
        for peer in ang_peers:
            ray_copy(c, peer, peer).wait_recv()
        total_rays[c] = dot(selector[...], ray_in[c].reshape(angles * hit_rows, slices))
        for k in range(strips):
            dense_out[c, k] = total_rays[c, k * columns:(k + 1) * columns].astype(jnp.bfloat16)
        for peer in strip_peers:
            start(dense_copy(c, strip, peer))

    middle = frames // 4 * 2
    for pair in range(0, middle, 2):
        frame_pair(pair)
    sum_rays(0)
    for pair in range(middle, frames, 2):
        frame_pair(pair)
    deposit = one_hot(detector, [positions[j] for j in range(frames)], frames, side, 1)
    high, low = split(grads[...])
    deposited = dot(deposit, high) + dot(deposit, low)
    for c in range(chunks):
        total_grad[c] = deposited[:, c * slices:(c + 1) * slices]
        for k in range(strips):
            grad_out[c, k] = total_grad[c, k * columns:(k + 1) * columns].astype(jnp.bfloat16)
        for peer in strip_peers:
            start(grad_copy(c, strip, peer))
    for c in range(1, chunks):
        sum_rays(c)
    for k in range(angles):
        picker[k] = window(ranges[k] * RAYS, hit_rows, detector)

    for c in range(chunks):
        intersection = total_grad[c, rows_of(strip), :]
        for peer in strip_peers:
            grad_copy(c, peer, peer).wait_recv()
            intersection = intersection + grad_in[c, peer].astype(jnp.float32)
        projection = total_rays[c, rows_of(strip), :]
        for peer in strip_peers:
            dense_copy(c, peer, peer).wait_recv()
            projection = projection + dense_in[c, peer].astype(jnp.float32)
        part = pl.ds(c, columns, stride=chunks)
        part_field, part_dual = field[part, :], dual[part, :]
        updated = part_field - object_step * (
            intersection + part_dual + penalty * (part_field - projection)
        )
        residual = penalty * (projection - updated) - part_dual
        rows_half[c, rows_of(strip), :] = residual.astype(jnp.bfloat16)
        for peer in strip_peers:
            start(residual_copy(c, strip, peer))
        object_next[part, :] = updated
        dual_next[part, :] = part_dual + penalty * (updated - projection)
    for c in range(chunks):
        for peer in strip_peers:
            residual_copy(c, peer, peer).wait_recv()
        rows = rows_half[c]
        for peer in ang_peers:
            pick_out[c, peer] = dot(picker[peer], rows).astype(jnp.bfloat16)
            start(pick_copy(c, me, peer))
        pick_in[c, me] = dot(picker[me], rows).astype(jnp.bfloat16)
    turned_radon[...] = radon[...].T
    for c in range(chunks):
        for peer in ang_peers:
            pick_copy(c, peer, peer).wait_recv()
        gradient = dot(turned_radon[...], pick_in[c].reshape(angles * hit_rows, slices))
        part = pl.ds(c, pixels, stride=chunks)
        volume_next[part, :] = volume[part, :] - volume_step * gradient
    for copy in started:
        copy.wait_send()


def body(
    measured, positions, probe_field, object_field, dual_field, volume, radon_tiles, tile_range
):
    angles, strips = lax.axis_size("ang"), lax.axis_size("strip")
    frames, side = measured.shape[1], measured.shape[2]
    columns, width = object_field.shape[1], object_field.shape[2] * object_field.shape[3]
    hit_rows = radon_tiles.shape[2] * radon_tiles.shape[3]
    pixels = radon_tiles.shape[4]
    chunks, slices = object_field.shape[2], object_field.shape[3]
    vmem = pl.BlockSpec(memory_space=pltpu.VMEM)
    smem = pl.BlockSpec(memory_space=pltpu.SMEM)
    half = jnp.bfloat16
    outs = pl.pallas_call(
        functools.partial(kernel, angles, strips),
        out_shape=(
            jax.ShapeDtypeStruct((2 * columns, slices), jnp.float32),
            jax.ShapeDtypeStruct((2 * columns, slices), jnp.float32),
            jax.ShapeDtypeStruct((2 * pixels, slices), jnp.float32),
        ),
        in_specs=[smem, smem] + [pl.BlockSpec(memory_space=pltpu.HBM)] * 7,
        out_specs=(vmem, vmem, vmem),
        scratch_shapes=[
            pltpu.VMEM((frames, side, side), jnp.float32),
            pltpu.VMEM((chunks, side, side), jnp.float32),
            pltpu.VMEM((chunks * columns, slices), jnp.float32),
            pltpu.VMEM((chunks * columns, slices), jnp.float32),
            pltpu.VMEM((chunks * pixels, slices), jnp.float32),
            pltpu.VMEM((angles * hit_rows, pixels), half),
            pltpu.VMEM((4, side, side), half),
        ] + [pltpu.VMEM((chunks, angles, hit_rows, slices), half)] * 4 + [
            pltpu.VMEM((columns, width), half),
            pltpu.VMEM((strips, columns, width), half),
        ] + [pltpu.VMEM((chunks, strips, columns, slices), half)] * 4 + [
            pltpu.VMEM((chunks, strips * columns, slices), half),
            pltpu.VMEM((strips * columns, width), jnp.float32),
            pltpu.VMEM((frames * side, width), jnp.float32),
            pltpu.VMEM((chunks, strips * columns, slices), jnp.float32),
            pltpu.VMEM((chunks, strips * columns, slices), jnp.float32),
            pltpu.VMEM((pixels, angles * hit_rows), half),
            pltpu.VMEM((angles, hit_rows, strips * columns), half),
            pltpu.VMEM((strips * columns, angles * hit_rows), half),
            pltpu.SemaphoreType.DMA((7,)),
        ] + [pltpu.SemaphoreType.DMA((chunks, angles))] * 4
        + [pltpu.SemaphoreType.DMA((1 + 3 * chunks, strips))] * 2,
        compiler_params=pltpu.CompilerParams(
            collective_id=0, has_side_effects=True, vmem_limit_bytes=VMEM_BYTES
        ),
    )(
        positions.reshape(frames),
        tile_range.reshape(angles),
        measured[0],
        probe_field,
        object_field.reshape(2 * columns, slices),
        dual_field.reshape(2 * columns, slices),
        volume.reshape(2 * pixels, slices),
        radon_tiles.reshape(angles * hit_rows, pixels),
        jnp.asarray(dft_tables(side)),
    )
    return (
        outs[0].reshape(object_field.shape),
        outs[1].reshape(dual_field.shape),
        outs[2].reshape(volume.shape),
    )


def solution(mesh):
    return jax.shard_map(
        body,
        mesh=mesh,
        in_specs=(
            P("ang", "strip", None, None),
            P("ang", "strip"),
            P(),
            P("ang", "strip", None, None),
            P("ang", "strip", None, None),
            P(("ang", "strip"), None, None),
            P(("ang", "strip"), None, None, None, None),
            P("ang", None, "strip", None),
        ),
        out_specs=(
            P("ang", "strip", None, None),
            P("ang", "strip", None, None),
            P(("ang", "strip"), None, None),
        ),
        check_vma=False,
    )
```

time: 52.5 us -> 46.1 us (0.88)
  local copies, waits for them, and re-layouts: 9.5 us -> 3.46 us
    unnamed x21 -> x7, local copies, waits for them, and re-layouts: 9.5 us -> 3.46 us
where the time goes in v2:
time: 46.1 us; the launch traced here: 45.9 us
  Pallas kernels  41.8 us (91%)
  local copies, waits for them, and re-layouts  3.46 us (8%)
  between operations  0.65 us (1%)
    pallas_call x1, Pallas kernels, body(): pl.pallas_call(functools.partial(kernel, angles, strips), out_shape=(jax....  41.8 us
    unnamed x7, local copies, waits for them, and re-layouts  3.46 us

profile of v2, /device:TPU:0, one launch (start us, length us, event | category | flops | bytes accessed | tf_op | source)
XLA Modules:
  0.0 45.9 jit_solution(15059019979179958499)
XLA Ops:
  0.6 41.8 %shard_map.112 = (f32[512,128]{1,0:T(8,128)}, f32[512,128]{1,0:T(8,128)}, f32[512,128]{1,0:T(8,128)}) custom-call(s32[8]{0:T(128)} %bitcast.18, s32[16]{0:T(128)} %bitcast.19, f32[8,128,128]{2,1,0:T(8,128)} %bitcast.10, f32[2,128,128]{2,1,0:T(8,128)} %probe_hbm.1, f32[512,128]{1,0:T(8,128)} %bitcast.15, f32[512,128]{1,0:T(8,128)} %bitcast.16, ...), custom_call_target="tpu_custom_call" | custom-call | tf_op jit(solution)/shard_map/pallas_call | solution.py:321
  42.4 0.0 copy-start.1
  42.4 1.7 %copy.15 = f32[1,256,2,128]{3,2,1,0:T(2,128)} copy(f32[1,256,2,128]{3,2,1,0:T(2,128)} %bitcast.14) | data formatting | bytes 524288
  44.2 0.0 copy-done.1
  44.2 0.0 copy-start
  44.2 0.7 %copy.16 = f32[1,256,2,128]{3,2,1,0:T(2,128)} copy(f32[1,256,2,128]{3,2,1,0:T(2,128)S(1)} %bitcast.13) | data formatting | bytes 524288
  44.9 0.3 copy-done
  45.2 0.7 %copy.17 = f32[256,2,128]{2,1,0:T(2,128)} copy(f32[256,2,128]{2,1,0:T(2,128)S(1)} %bitcast.12) | data formatting | bytes 524288
Async XLA Ops:
  42.4 1.7 %copy-start.1 = (f32[512,128]{1,0:T(8,128)S(1)}, f32[512,128]{1,0:T(8,128)}, u32[]{:S(2)}) copy-start(f32[512,128]{1,0:T(8,128)} %get-tuple-element.7) | copy-start | bytes 786436
  44.2 1.0 %copy-start = (f32[512,128]{1,0:T(8,128)S(1)}, f32[512,128]{1,0:T(8,128)}, u32[]{:S(2)}) copy-start(f32[512,128]{1,0:T(8,128)} %get-tuple-element.8) | copy-start | bytes 786436
